TPU v7x, 32 devices: a whole 2x2x4 slice. The times are simulated.
32 devices in a mesh: band: 8 (over z, y), pair: 4 (over x, core).
Axes of the slice: x: 2, y: 2, z: 4, core: 2. Of those that a mesh axis runs over, the one named last changes fastest.
Arguments:
- orbitals: bfloat16 [32, 262144], P(('band', 'pair')), may hold values from -64 to 64
- partners: int32 [32, 3], P(('band', 'pair')), may hold values from -1 to 31, as said below
Outputs:
- gradient: float32 [32, 262144], P(None, ('band', 'pair'))
Inputs may be any that keep to these rules, and one draw needn't show every extreme that they name: `partners`: slot k of orbital i holds either -1 or i XOR (4 * 2**k); j is listed by i exactly when i is listed by j.
All inputs are finite; a program needn't handle non-finite values.
Results may differ from a plain program's by a relative error of at most 0.0008.
The roundings to bfloat16 on the way count: a program that leaves them out, or rounds other values in their place, can miss the bound.
Values may be sent and summed in bfloat16 or wider, within the bound.
A program may use at most 64 MiB of HBM per device.

v0:
```python
import functools

import jax
import jax.numpy as jnp
import numpy as np
from jax import lax
from jax.experimental import pallas as pl
from jax.experimental.pallas import tpu as pltpu
from jax.sharding import PartitionSpec as P

screening = 0.05
GROUP = 8
MESH = pl.DeviceIdType.MESH


def halves(table):
    high = table.astype(np.float32).astype(jnp.bfloat16)
    low = (table - high.astype(np.float64)).astype(jnp.bfloat16)
    return np.asarray(high), np.asarray(low)


def tables(size):
    index = np.arange(size) + 1
    product = index[:, None] * index[None, :] % (2 * (size + 1))
    sine = np.sqrt(2.0 / (size + 1)) * np.sin(np.pi * product / (size + 1))
    half = size // 2
    high, low = halves(sine)
    left = np.block([[high, high], [low, low]])
    high, low = halves(np.kron(np.eye(2), sine))
    right = np.block([[high, low], [high, low]])
    even, odd = sine[:half, 0::2], sine[:half, 1::2]
    high, low = halves(np.concatenate([even, odd], axis=1))
    forth = np.block([[high, high], [low, low]])
    high, low = halves(np.concatenate([even.T, odd.T], axis=1))
    back = np.block([[high, high], [low, low]])
    lam = 2.0 - 2.0 * np.cos(np.pi * index / (size + 1))
    pair = np.concatenate(
        [lam[:half, None] + lam[None, :], lam[::-1][:half, None] + lam[None, :]], axis=1
    )
    pair = (pair + screening).astype(np.float32)
    along = np.broadcast_to(lam.astype(np.float32)[:, None], (size, 2 * size)).copy()
    return left, right, forth, back, pair, along


def split(value, axis):
    high = value.astype(jnp.bfloat16)
    low = (value - high.astype(jnp.float32)).astype(jnp.bfloat16)
    return jnp.concatenate([high, low], axis=axis)


def dot(a, b):
    return jnp.dot(a, b, preferred_element_type=jnp.float32)


def stacked(value, lanes):
    return jnp.concatenate(
        [value[:, at : at + lanes] for at in range(0, value.shape[1], lanes)], axis=0
    )


def spread(value, rows):
    return jnp.concatenate(
        [value[at : at + rows] for at in range(0, value.shape[0], rows)], axis=1
    )


def solve(density, work, left, right, forth, back, pair, along):
    lanes = density.shape[1]
    size, half = lanes // 2, lanes // 4
    lane = lax.broadcasted_iota(jnp.int32, (half, GROUP * lanes), 1) % lanes
    first = lane < size
    sign = jnp.where(
        lax.broadcasted_iota(jnp.int32, (GROUP * half, lanes), 1) < size, 1.0, -1.0
    ).astype(jnp.float32)

    def planes(source, start):
        field = jnp.concatenate(
            [source[pl.ds(start + i, size, stride=half), :] for i in range(GROUP)], axis=1
        )
        field = dot(left[...], split(field, 0))
        field = stacked(field[:size] + field[size:], lanes)
        field = dot(split(field, 1), right[...])
        return field[:, :lanes] + field[:, lanes:]

    def middle(table, field):
        field = jnp.concatenate(
            [jnp.where(first, field, 0.0), jnp.where(first, 0.0, field)], axis=0
        )
        field = dot(table[...], split(field, 0))
        return stacked(field[:half] + field[half:], lanes)

    def fold(field):
        return pltpu.roll(field, size, 1) + field * sign

    for start in range(0, half, GROUP):
        work[start * size : (start + GROUP) * size, :] = planes(density, start)
    for start in range(0, size, GROUP):
        field = jnp.concatenate(
            [work[pl.ds(start + i, half, stride=size), :] for i in range(GROUP)], axis=1
        )
        field = fold(middle(forth, field))
        denom = jnp.concatenate(
            [pair[...] + along[start + i : start + i + 1, :] for i in range(GROUP)], axis=0
        )
        field = middle(back, spread(fold(field / denom), half))
        density[start * half : (start + GROUP) * half, :] = field
    for start in range(0, half, GROUP):
        field = planes(density, start)
        for i in range(GROUP):
            work[pl.ds(start + i, size, stride=half), :] = field[i * size : (i + 1) * size]


def slot_kernel(slot, last, live, own, other, *refs):
    earlier, refs = refs[: 2 * last], refs[2 * last :]
    left, right, forth, back, pair, along, out, density, work = refs

    @pl.when(live[slot] >= 0)
    def _():
        density[...] = own[...].astype(jnp.float32) * other[...].astype(jnp.float32)
        solve(density, work, left, right, forth, back, pair, along)
        term = (work[...] * other[...].astype(jnp.float32)).astype(jnp.bfloat16)
        if last:
            total = earlier[0][...].astype(jnp.float32) + earlier[1][...].astype(jnp.float32)
            term = (total + term.astype(jnp.float32)).astype(jnp.bfloat16)
        out[...] = term

    @pl.when(live[slot] < 0)
    def _():
        if last:
            total = earlier[0][...].astype(jnp.float32) + earlier[1][...].astype(jnp.float32)
            out[...] = total.astype(jnp.bfloat16)
        else:
            out[...] = jnp.zeros_like(out)


def slot_term(slot, live, own, other, earlier, consts):
    vmem = pl.BlockSpec(memory_space=pltpu.VMEM)
    rows, lanes = own.shape
    return pl.pallas_call(
        functools.partial(slot_kernel, slot, 1 if earlier else 0),
        out_shape=jax.ShapeDtypeStruct(own.shape, jnp.bfloat16),
        in_specs=[pl.BlockSpec(memory_space=pltpu.SMEM)] + [vmem] * (2 + len(earlier) + len(consts)),
        out_specs=vmem,
        scratch_shapes=[pltpu.VMEM((rows, lanes), jnp.float32)] * 2,
        cost_estimate=pl.CostEstimate(
            flops=24 * rows * lanes * lanes * 8, bytes_accessed=6 * rows * lanes, transcendentals=0
        ),
        name=f"slot{slot}",
    )(live, own, other, *earlier, *consts)


def place(index):
    pairs = lax.axis_size("pair")
    return (index // pairs, index % pairs)


def remove_kernel(count, cells, scale, applied, phi, out, slab, wide, sums, sent, came, sent2, came2, here):
    rows, lanes = slab.shape[1:]
    me = lax.axis_index("band") * lax.axis_size("pair") + lax.axis_index("pair")

    def regroup(step):
        peer = lax.rem(me + step, count)
        return pltpu.make_async_remote_copy(
            src_ref=applied.at[peer], dst_ref=slab.at[me], send_sem=sent.at[step],
            recv_sem=came.at[step], device_id=place(peer), device_id_type=MESH,
        )

    def share(step):
        peer = lax.rem(me + step, count)
        return pltpu.make_async_remote_copy(
            src_ref=sums.at[me], dst_ref=sums.at[me], send_sem=sent2.at[step],
            recv_sem=came2.at[step], device_id=place(peer), device_id_type=MESH,
        )

    def each(action):
        lax.fori_loop(1, count, lambda step, _: (action(step), 0)[1], 0)

    each(lambda step: regroup(step).start())
    own = pltpu.make_async_copy(applied.at[me], slab.at[me], here)
    own.start()
    own.wait()
    each(lambda step: regroup(step).wait())
    wide[...] = slab[...].reshape(count * rows, lanes).astype(jnp.float32)
    for row in range(rows):
        out[:, row * lanes : (row + 1) * lanes] = wide[pl.ds(row, count, stride=rows), :]
    partial = lax.dot_general(
        phi[...], out[...].astype(jnp.bfloat16), (((1,), (1,)), ((), ())),
        preferred_element_type=jnp.float32,
    ) * scale
    short = count * count // lanes
    sums[me] = jnp.concatenate(
        [partial[at : at + short] for at in range(0, count, short)], axis=1
    )
    each(lambda step: share(step).start())
    each(lambda step: share(step).wait())
    packed = jnp.sum(sums[...], axis=0)
    total = jnp.concatenate(
        [packed[:, at : at + count] for at in range(0, lanes, count)], axis=0
    )
    removed = lax.dot_general(
        total, phi[...].astype(jnp.float32), (((0,), (0,)), ((), ())),
        precision=lax.Precision.HIGHEST, preferred_element_type=jnp.float32,
    )
    out[...] = out[...] - removed


def regrouped(value, count):
    bands, pairs = lax.axis_size("band"), lax.axis_size("pair")
    rows, lanes = value.shape
    value = value.reshape(bands, pairs, rows // count, lanes)
    value = lax.all_to_all(value, "band", split_axis=0, concat_axis=0, tiled=True)
    value = lax.all_to_all(value, "pair", split_axis=1, concat_axis=1, tiled=True)
    return value.reshape(count, rows * lanes // count)


def on_device(orbitals, partners):
    cells = orbitals.shape[1]
    size = round(cells ** (1.0 / 3.0))
    lanes = 2 * size
    count = lax.axis_size("band") * lax.axis_size("pair")
    consts = [jnp.asarray(table) for table in tables(size)]
    own = orbitals.reshape(cells // lanes, lanes)
    live = partners[0]
    arrived = []
    for slot in range(partners.shape[1]):
        pairs = [(source, source ^ 2**slot) for source in range(lax.axis_size("band"))]
        arrived.append(lax.ppermute(own, "band", pairs))
    terms = []
    for slot in range(2):
        terms.append(slot_term(slot, live, own, arrived[slot], [], consts))
    applied = slot_term(2, live, own, arrived[2], terms, consts)
    phi = regrouped(own, count)
    scale = 1.0 / cells
    slab = cells // count
    if slab % (8 * lanes) or count * count % (8 * lanes):
        other = regrouped(applied, count)
        partial = lax.dot_general(
            phi, other, (((1,), (1,)), ((), ())), preferred_element_type=jnp.float32
        )
        total = lax.psum(partial * scale, ("band", "pair"))
    elif count * count * count * 4 > 2**24:
        other = regrouped(applied, count)
        partial = lax.dot_general(
            phi, other, (((1,), (1,)), ((), ())), preferred_element_type=jnp.float32
        )
        total = lax.psum(partial * scale, ("band", "pair"))
    else:
        vmem = pl.BlockSpec(memory_space=pltpu.VMEM)
        rows = slab // lanes
        return pl.pallas_call(
            functools.partial(remove_kernel, count, cells, scale),
            out_shape=jax.ShapeDtypeStruct((count, slab), jnp.float32),
            in_specs=[vmem, vmem],
            out_specs=vmem,
            scratch_shapes=[
                pltpu.VMEM((count, rows, lanes), jnp.bfloat16),
                pltpu.VMEM((count * rows, lanes), jnp.float32),
                pltpu.VMEM((count, count * count // lanes, lanes), jnp.float32),
                pltpu.SemaphoreType.DMA((count,)),
                pltpu.SemaphoreType.DMA((count,)),
                pltpu.SemaphoreType.DMA((count,)),
                pltpu.SemaphoreType.DMA((count,)),
                pltpu.SemaphoreType.DMA,
            ],
            compiler_params=pltpu.CompilerParams(has_side_effects=True),
            name="remove",
        )(applied.reshape(count, rows, lanes), phi)
    removed = lax.dot_general(
        total, phi.astype(jnp.float32), (((0,), (0,)), ((), ())), precision=lax.Precision.HIGHEST
    )
    return other.astype(jnp.float32) - removed


def solution(mesh):
    placed = (P(("band", "pair"), None), P(("band", "pair"), None))
    return jax.shard_map(
        on_device, mesh=mesh, in_specs=placed, out_specs=P(None, ("band", "pair")), check_vma=False
    )
```

profile of v0, /device:TPU:0, one launch (start us, length us, event | category | flops | bytes accessed | tf_op | source)
XLA Modules:
  0.0 101.5 jit_solution(15299386270056214648)
XLA Ops:
  0.0 12.7 %reduce = bf16[262144]{0:T(1024)(128)(2,1)} reduce(bf16[1,262144]{1,0:T(2,128)(2,1)} %param.8, bf16[]{:T(256)} %constant.20), dimensions={0}, to_apply=%param.8.reduce_sub_computation | reduce | bytes 1048578 | tf_op args[0]
  12.7 3.0 %collective-permute-start.1 = (bf16[2048,128]{1,0:T(8,128)(2,1)}, bf16[2048,128]{1,0:T(8,128)(2,1)S(1)}, u32[]{:S(2)}, u32[]{:S(2)}) collective-permute-start(bf16[2048,128]{1,0:T(8,128)(2,1)} %bitcast.2.own), channel_id=1, source_target_pairs={{0,4},{4,0},{8,12},{12,8},{16,20},{20,16},{24,28},{28,24},{1,5},{5... | collective-permute-start | bytes 1572872 | tf_op jit(solution)/shard_map/ppermute | solution.py:227
  15.7 1.6 %collective-permute-start.2 = (bf16[2048,128]{1,0:T(8,128)(2,1)}, bf16[2048,128]{1,0:T(8,128)(2,1)S(1)}, u32[]{:S(2)}, u32[]{:S(2)}) collective-permute-start(bf16[2048,128]{1,0:T(8,128)(2,1)} %bitcast.2.own), channel_id=1, source_target_pairs={{0,8},{4,12},{8,0},{12,4},{16,24},{20,28},{24,16},{28,20},{1,9},{5... | collective-permute-start | bytes 1572872 | tf_op jit(solution)/shard_map/ppermute | solution.py:227
  17.3 2.6 %collective-permute-start = (bf16[2048,128]{1,0:T(8,128)(2,1)}, bf16[2048,128]{1,0:T(8,128)(2,1)S(1)}, u32[]{:S(2)}, u32[]{:S(2)}) collective-permute-start(bf16[2048,128]{1,0:T(8,128)(2,1)} %bitcast.2.own), channel_id=1, source_target_pairs={{0,16},{4,20},{8,24},{12,28},{16,0},{20,4},{24,8},{28,12},{1,17},{... | collective-permute-start | bytes 1572872 | tf_op jit(solution)/shard_map/ppermute | solution.py:227
  19.9 3.5 %all-to-all-start = ((bf16[8,4,64,128]{3,2,1,0:T(8,128)(2,1)}), bf16[8,4,64,128]{3,2,1,0:T(8,128)(2,1)S(1)}, u32[]{:S(2)}, u32[]{:S(2)}) async-start(bf16[8,4,64,128]{3,2,1,0:T(8,128)(2,1)} %bitcast.3), calls=%async_computation | async-start | bytes 1048576 | tf_op jit(solution)/shard_map/all_to_all | solution.py:211
  23.4 5.2 %collective-permute-done.1.other = bf16[2048,128]{1,0:T(8,128)(2,1)S(1)} collective-permute-done((bf16[2048,128]{1,0:T(8,128)(2,1)}, bf16[2048,128]{1,0:T(8,128)(2,1)S(1)}, u32[]{:S(2)}, u32[]{:S(2)}) %collective-permute-start.1) | collective-permute-done | bytes 524320 | tf_op jit(solution)/shard_map/ppermute | solution.py:227
  28.5 0.0 copy-start.2
  28.5 0.8 copy-done.2
  29.3 8.1 %slot0.1.refs_0_ = bf16[2048,128]{1,0:T(8,128)(2,1)} custom-call(s32[3]{0:T(128)} %bitcast.12, bf16[2048,128]{1,0:T(8,128)(2,1)} %bitcast.2.own, bf16[2048,128]{1,0:T(8,128)(2,1)} %copy-done.2, bf16[128,128]{1,0:T(8,128)(2,1)} %constant.12.clone.refs_0_.refs_2_, bf16[256,256]{1,0:T(8,128)(2,1)} %constant.13.clone.refs_1_.refs_3_, ...), custom_call_target="tpu_custom_call" | custom-call | flops 6442450944 | bytes 1572864 | tf_op jit(solution)/shard_map/slot0/pallas_call | solution.py:139
  37.4 3.6 %collective-permute-done.2.other = bf16[2048,128]{1,0:T(8,128)(2,1)S(1)} collective-permute-done((bf16[2048,128]{1,0:T(8,128)(2,1)}, bf16[2048,128]{1,0:T(8,128)(2,1)S(1)}, u32[]{:S(2)}, u32[]{:S(2)}) %collective-permute-start.2) | collective-permute-done | bytes 524320 | tf_op jit(solution)/shard_map/ppermute | solution.py:227
  41.0 0.0 copy-start.1
  41.1 0.8 copy-done.1
  41.9 8.3 %slot1.1.refs_1_ = bf16[2048,128]{1,0:T(8,128)(2,1)} custom-call(s32[3]{0:T(128)} %bitcast.13, bf16[2048,128]{1,0:T(8,128)(2,1)} %bitcast.2.own, bf16[2048,128]{1,0:T(8,128)(2,1)} %copy-done.1, bf16[128,128]{1,0:T(8,128)(2,1)} %constant.12.clone.refs_0_.refs_2_, bf16[256,256]{1,0:T(8,128)(2,1)} %constant.13.clone.refs_1_.refs_3_, ...), custom_call_target="tpu_custom_call" | custom-call | flops 6442450944 | bytes 1572864 | tf_op jit(solution)/shard_map/slot1/pallas_call | solution.py:139
  50.1 3.9 %all-to-all-done = bf16[8,4,64,128]{3,2,1,0:T(8,128)(2,1)S(1)} async-done(((bf16[8,4,64,128]{3,2,1,0:T(8,128)(2,1)}), bf16[8,4,64,128]{3,2,1,0:T(8,128)(2,1)S(1)}, u32[]{:S(2)}, u32[]{:S(2)}) %all-to-all-start) | async-done | bytes 524320 | tf_op jit(solution)/shard_map/all_to_all | solution.py:211
  54.0 0.8 copy.10
  54.9 3.5 %all-to-all-start.1 = ((bf16[8,4,64,128]{3,2,0,1:T(8,128)(2,1)}), bf16[8,4,64,128]{3,2,0,1:T(8,128)(2,1)S(1)}, u32[]{:S(2)}, u32[]{:S(2)}) async-start(bf16[8,4,64,128]{3,2,0,1:T(8,128)(2,1)} %copy.10), calls=%async_computation.1 | async-start | bytes 1048576 | tf_op jit(solution)/shard_map/all_to_all | solution.py:212
  58.3 0.0 collective-permute-done.other
  58.3 0.0 copy-start
  58.4 0.8 copy-done
  59.1 8.6 %slot2.1 = bf16[2048,128]{1,0:T(8,128)(2,1)} custom-call(s32[3]{0:T(128)} %bitcast.14, bf16[2048,128]{1,0:T(8,128)(2,1)} %bitcast.2.own, bf16[2048,128]{1,0:T(8,128)(2,1)} %copy-done, bf16[2048,128]{1,0:T(8,128)(2,1)} %slot0.1.refs_0_, bf16[2048,128]{1,0:T(8,128)(2,1)} %slot1.1.refs_1_, bf16[128,128]{1,0:T(8,128)(2,1)} %constant.12.clone.refs_0_.refs_2_, ...), custom_call_target="tpu_custom_call" | custom-call | flops 6442450944 | bytes 1572864 | tf_op jit(solution)/shard_map/slot2/pallas_call | solution.py:139
  67.7 0.0 all-to-all-done.1
  67.7 1.1 %copy.14 = bf16[4,8,64,128]{3,1,2,0:T(8,128)(2,1)} copy(bf16[4,8,64,128]{3,2,1,0:T(8,128)(2,1)S(1)} %bitcast.9) | data formatting | bytes 1048576
  68.9 30.4 %remove.1 = f32[32,8192]{1,0:T(8,128)} custom-call(bf16[32,64,128]{2,1,0:T(8,128)(2,1)} %bitcast.11, bf16[32,8192]{1,0:T(8,128)(2,1)} %bitcast.10), custom_call_target="tpu_custom_call" | custom-call | tf_op jit(solution)/shard_map/remove/pallas_call | solution.py:250
  99.3 2.3 %copy.16 = f32[32,8192]{1,0:T(8,128)} copy(f32[32,8192]{1,0:T(8,128)} %remove.1) | data formatting | bytes 2097152
  (1 shorter events, 0.0 us)
Async XLA Ops:
  12.7 15.8 %collective-permute-start.1 = (bf16[2048,128]{1,0:T(8,128)(2,1)}, bf16[2048,128]{1,0:T(8,128)(2,1)S(1)}, u32[]{:S(2)}, u32[]{:S(2)}) collective-permute-start(bf16[2048,128]{1,0:T(8,128)(2,1)} %bitcast.2.own), channel_id=1, source_target_pairs={{0,4},{4,0},{8,12},{12,8},{16,20},{20,16},{24,28},{28,24},{1,5},{5... | collective-permute-start | bytes 1572872 | tf_op jit(solution)/shard_map/ppermute | solution.py:227
  15.7 25.4 %collective-permute-start.2 = (bf16[2048,128]{1,0:T(8,128)(2,1)}, bf16[2048,128]{1,0:T(8,128)(2,1)S(1)}, u32[]{:S(2)}, u32[]{:S(2)}) collective-permute-start(bf16[2048,128]{1,0:T(8,128)(2,1)} %bitcast.2.own), channel_id=1, source_target_pairs={{0,8},{4,12},{8,0},{12,4},{16,24},{20,28},{24,16},{28,20},{1,9},{5... | collective-permute-start | bytes 1572872 | tf_op jit(solution)/shard_map/ppermute | solution.py:227
  17.3 41.1 %collective-permute-start = (bf16[2048,128]{1,0:T(8,128)(2,1)}, bf16[2048,128]{1,0:T(8,128)(2,1)S(1)}, u32[]{:S(2)}, u32[]{:S(2)}) collective-permute-start(bf16[2048,128]{1,0:T(8,128)(2,1)} %bitcast.2.own), channel_id=1, source_target_pairs={{0,16},{4,20},{8,24},{12,28},{16,0},{20,4},{24,8},{28,12},{1,17},{... | collective-permute-start | bytes 1572872 | tf_op jit(solution)/shard_map/ppermute | solution.py:227
  19.9 34.2 %all-to-all-start = ((bf16[8,4,64,128]{3,2,1,0:T(8,128)(2,1)}), bf16[8,4,64,128]{3,2,1,0:T(8,128)(2,1)S(1)}, u32[]{:S(2)}, u32[]{:S(2)}) async-start(bf16[8,4,64,128]{3,2,1,0:T(8,128)(2,1)} %bitcast.3), calls=%async_computation | async-start | bytes 1048576 | tf_op jit(solution)/shard_map/all_to_all | solution.py:211
  28.5 0.8 copy-start.2
  41.0 0.8 copy-start.1
  54.9 12.8 %all-to-all-start.1 = ((bf16[8,4,64,128]{3,2,0,1:T(8,128)(2,1)}), bf16[8,4,64,128]{3,2,0,1:T(8,128)(2,1)S(1)}, u32[]{:S(2)}, u32[]{:S(2)}) async-start(bf16[8,4,64,128]{3,2,0,1:T(8,128)(2,1)} %copy.10), calls=%async_computation.1 | async-start | bytes 1048576 | tf_op jit(solution)/shard_map/all_to_all | solution.py:212
  58.3 0.8 copy-start
where the time goes:
time: 102 us
  Pallas kernels  55.3 us (54%)
  starting transfers between devices  14.1 us (14%)
  other arithmetic  12.7 us (12%)
  waiting for transfers between devices  12.7 us (12%)
  local copies, waits for them, and re-layouts  6.67 us (7%)
    pallas_call x1, Pallas kernels, on_device(): pl.pallas_call(functools.partial(remove_kernel, count, cells, scale), out...  30.4 us
    pallas_call x3, Pallas kernels, slot_term(): pl.pallas_call(functools.partial(slot_kernel, slot, 1 if earlier else 0),...  24.9 us
    unnamed x1, other arithmetic  12.7 us
    ppermute x3, waiting for transfers between devices, on_device(): arrived.append(lax.ppermute(own, 'band', pairs))  8.79 us
    ppermute x3, starting transfers between devices, on_device(): arrived.append(lax.ppermute(own, 'band', pairs))  7.16 us
    unnamed x8, local copies, waits for them, and re-layouts  5.79 us
    all_to_all x1, waiting for transfers between devices, regrouped(): lax.all_to_all(value, 'band', split_axis=0, concat_axis=0, tiled=True)  3.88 us
    all_to_all x1, starting transfers between devices, regrouped(): lax.all_to_all(value, 'band', split_axis=0, concat_axis=0, tiled=True)  3.49 us
  transfers between devices with their start and end apart: 5, of which 3 were waited for; matrix products, arithmetic and copies ran while one was open for 1% of the time, Pallas kernels for 25%

commit v1 on v0

v1 whole, which is shorter than its diff:
```python
import functools

import jax
import jax.numpy as jnp
import numpy as np
from jax import lax
from jax.experimental import pallas as pl
from jax.experimental.pallas import tpu as pltpu
from jax.sharding import PartitionSpec as P

screening = 0.05
GROUP = 8
MESH = pl.DeviceIdType.MESH


def halves(table):
    high = table.astype(np.float32).astype(jnp.bfloat16)
    low = (table - high.astype(np.float64)).astype(jnp.bfloat16)
    return np.asarray(high), np.asarray(low)


def tables(size):
    index = np.arange(size) + 1
    product = index[:, None] * index[None, :] % (2 * (size + 1))
    sine = np.sqrt(2.0 / (size + 1)) * np.sin(np.pi * product / (size + 1))
    half = size // 2
    high, low = halves(sine)
    left = np.block([[high, high], [low, low]])
    high, low = halves(np.kron(np.eye(2), sine))
    right = np.block([[high, low], [high, low]])
    even, odd = sine[:half, 0::2], sine[:half, 1::2]
    high, low = halves(np.concatenate([even, odd], axis=1))
    forth = np.block([[high, high], [low, low]])
    high, low = halves(np.concatenate([even.T, odd.T], axis=1))
    back = np.block([[high, high], [low, low]])
    lam = 2.0 - 2.0 * np.cos(np.pi * index / (size + 1))
    pair = np.concatenate(
        [lam[:half, None] + lam[None, :], lam[::-1][:half, None] + lam[None, :]], axis=1
    )
    pair = (pair + screening).astype(np.float32)
    along = np.broadcast_to(lam.astype(np.float32)[:, None], (size, 2 * size)).copy()
    return left, right, forth, back, pair, along


def split(value, axis):
    high = value.astype(jnp.bfloat16)
    low = (value - high.astype(jnp.float32)).astype(jnp.bfloat16)
    return jnp.concatenate([high, low], axis=axis)


def dot(a, b):
    return jnp.dot(a, b, preferred_element_type=jnp.float32)


def stacked(value, lanes):
    return jnp.concatenate(
        [value[:, at : at + lanes] for at in range(0, value.shape[1], lanes)], axis=0
    )


def spread(value, rows):
    return jnp.concatenate(
        [value[at : at + rows] for at in range(0, value.shape[0], rows)], axis=1
    )


def middle(table, field, half):
    lanes = 4 * half
    lane = lax.broadcasted_iota(jnp.int32, field.shape, 1) % lanes
    first = lane < 2 * half
    field = jnp.concatenate([jnp.where(first, field, 0.0), jnp.where(first, 0.0, field)], axis=0)
    field = dot(table[...], split(field, 0))
    return stacked(field[:half] + field[half:], lanes)


def fold(field):
    size = field.shape[1] // 2
    sign = jnp.where(lax.broadcasted_iota(jnp.int32, field.shape, 1) < size, 1.0, -1.0)
    return pltpu.roll(field, size, 1) + field * sign.astype(jnp.float32)


def solve(own, other, work, consts):
    left, right, forth, back, pair, along = consts
    lanes = work.shape[1]
    size, half = lanes // 2, lanes // 4

    def across(field):
        field = dot(left[...], split(field, 0))
        return field[:size] + field[size:]

    def inner(field):
        field = dot(split(field, 1), right[...])
        return field[:, :lanes] + field[:, lanes:]

    for start in range(0, size, GROUP):
        rows = slice(start * half, (start + GROUP) * half)
        field = own[rows, :].astype(jnp.float32) * other[rows, :].astype(jnp.float32)
        work[rows, :] = fold(middle(forth, spread(field, half), half))
    for start in range(0, half, GROUP):
        field = jnp.concatenate(
            [work[pl.ds(start + i, size, stride=half), :] for i in range(GROUP)], axis=1
        )
        field = inner(stacked(across(field), lanes))
        denom = jnp.concatenate(
            [along[...] + pair[start + i : start + i + 1, :] for i in range(GROUP)], axis=0
        )
        field = across(spread(inner(field / denom), size))
        for i in range(GROUP):
            work[pl.ds(start + i, size, stride=half), :] = field[:, i * lanes : (i + 1) * lanes]


def finished(work, other, back, start):
    half = work.shape[1] // 4
    rows = slice(start * half, (start + GROUP) * half)
    field = middle(back, spread(fold(work[rows, :]), half), half)
    return rows, (field * other[rows, :].astype(jnp.float32)).astype(jnp.bfloat16)


def slot_kernel(slot, last, live, own, other, *refs):
    earlier, refs = refs[: 2 * last], refs[2 * last :]
    consts, out, work = refs[:6], refs[6], refs[7]
    solve(own, other, work, consts)
    for start in range(0, work.shape[1] // 2, GROUP):
        rows, term = finished(work, other, consts[3], start)
        term = jnp.where(live[slot] >= 0, term.astype(jnp.float32), 0.0)
        if last:
            total = earlier[0][rows, :].astype(jnp.float32) + earlier[1][rows, :].astype(jnp.float32)
            term = total + term
        out[rows, :] = term.astype(jnp.bfloat16)


def slot_term(slot, live, own, other, earlier, consts):
    vmem = pl.BlockSpec(memory_space=pltpu.VMEM)
    rows, lanes = own.shape
    return pl.pallas_call(
        functools.partial(slot_kernel, slot, 1 if earlier else 0),
        out_shape=jax.ShapeDtypeStruct(own.shape, jnp.bfloat16),
        in_specs=[pl.BlockSpec(memory_space=pltpu.SMEM)] + [vmem] * (2 + len(earlier) + len(consts)),
        out_specs=vmem,
        scratch_shapes=[pltpu.VMEM((rows, lanes), jnp.float32)],
        cost_estimate=pl.CostEstimate(
            flops=24 * rows * lanes * lanes * 8, bytes_accessed=6 * rows * lanes, transcendentals=0
        ),
        name=f"slot{slot}",
    )(live, own, other, *earlier, *consts)


def place(index):
    pairs = lax.axis_size("pair")
    return (index // pairs, index % pairs)


def whole_kernel(
    count, scale, live, orbital, *refs,
):
    consts, refs = refs[:6], refs[6:]
    out, own, other, terms, work, applied, slabs, phi, sums, slot_sems, sent, came = refs
    slots = other.shape[0]
    rows, lanes = slabs.shape[2:]
    band, pair = lax.axis_index("band"), lax.axis_index("pair")
    me = band * lax.axis_size("pair") + pair

    def each(action):
        lax.fori_loop(1, count, lambda step, _: (action(step), 0)[1], 0)

    def peer_of(step):
        return lax.rem(me + step, count)

    barrier = pltpu.get_barrier_semaphore()
    each(lambda step: pl.semaphore_signal(
        barrier, inc=1, device_id=place(peer_of(step)), device_id_type=MESH))
    grid = orbital[...].reshape(count * rows, lanes)
    own[...] = grid.reshape(count, rows, lanes)
    slabs[0, me] = own[me]
    pl.semaphore_wait(barrier, count - 1)

    def fetch(slot):
        stride = 2**slot
        mate = band + stride - 2 * stride * lax.rem(band // stride, 2)
        return pltpu.make_async_remote_copy(
            src_ref=own, dst_ref=other.at[slot], send_sem=slot_sems.at[0, slot],
            recv_sem=slot_sems.at[1, slot], device_id=(mate, pair), device_id_type=MESH,
        )

    def regroup(which, source):
        def copy(step):
            peer = peer_of(step)
            return pltpu.make_async_remote_copy(
                src_ref=source.at[peer], dst_ref=slabs.at[which, me],
                send_sem=sent.at[which, step], recv_sem=came.at[which, step],
                device_id=place(peer), device_id_type=MESH,
            )
        return copy

    def share(step):
        return pltpu.make_async_remote_copy(
            src_ref=sums.at[me], dst_ref=sums.at[me], send_sem=sent.at[2, step],
            recv_sem=came.at[2, step], device_id=place(peer_of(step)), device_id_type=MESH,
        )

    def widen(which):
        work[...] = slabs[which].reshape(count * rows, lanes).astype(jnp.float32)
        return [work[pl.ds(row, count, stride=rows), :] for row in range(rows)]

    fetches = [fetch(slot) for slot in range(slots)]
    for copy in fetches:
        copy.start()
    first, second = regroup(0, own), regroup(1, applied)
    each(lambda step: first(step).start())
    planes = lanes // 2
    flat = own.reshape(count * rows, lanes)
    for slot in range(slots):
        fetches[slot].wait()
        mate = other.at[slot].reshape(count * rows, lanes)
        solve(flat, mate, work, consts)
        for start in range(0, planes, GROUP):
            span, term = finished(work, mate, consts[3], start)
            term = jnp.where(live[0, slot] >= 0, term.astype(jnp.float32), 0.0)
            if slot + 1 < slots:
                terms[slot, span, :] = term.astype(jnp.bfloat16)
                continue
            total = terms[0, span, :].astype(jnp.float32)
            for earlier in range(1, slots - 1):
                total = total + terms[earlier, span, :].astype(jnp.float32)
            total = (total + term).astype(jnp.bfloat16)
            blocks = (span.stop - span.start) // rows
            at = span.start // rows
            applied[at : at + blocks] = total.reshape(blocks, rows, lanes)
    slabs[1, me] = applied[me]
    each(lambda step: second(step).start())
    each(lambda step: first(step).wait())
    for row, value in enumerate(widen(0)):
        phi[:, row * lanes : (row + 1) * lanes] = value.astype(jnp.bfloat16)
    each(lambda step: second(step).wait())
    for row, value in enumerate(widen(1)):
        out[:, row * lanes : (row + 1) * lanes] = value
    partial = lax.dot_general(
        phi[...], out[...].astype(jnp.bfloat16), (((1,), (1,)), ((), ())),
        preferred_element_type=jnp.float32,
    ) * scale
    short = count * count // lanes
    sums[me] = jnp.concatenate(
        [partial[at : at + short] for at in range(0, count, short)], axis=1
    )
    each(lambda step: share(step).start())
    each(lambda step: share(step).wait())
    packed = jnp.sum(sums[...], axis=0)
    total = jnp.concatenate(
        [packed[:, at : at + count] for at in range(0, lanes, count)], axis=0
    )
    removed = lax.dot_general(
        total, phi[...].astype(jnp.float32), (((0,), (0,)), ((), ())),
        precision=lax.Precision.HIGHEST, preferred_element_type=jnp.float32,
    )
    out[...] = out[...] - removed


def in_one_kernel(orbitals, partners, consts, count, lanes):
    cells = orbitals.shape[1]
    slots = partners.shape[1]
    slab = cells // count
    rows = slab // lanes
    vmem = pl.BlockSpec(memory_space=pltpu.VMEM)
    return pl.pallas_call(
        functools.partial(whole_kernel, count, 1.0 / cells),
        out_shape=jax.ShapeDtypeStruct((count, slab), jnp.float32),
        in_specs=[pl.BlockSpec(memory_space=pltpu.SMEM)] + [vmem] * (1 + len(consts)),
        out_specs=vmem,
        scratch_shapes=[
            pltpu.VMEM((count, rows, lanes), jnp.bfloat16),
            pltpu.VMEM((slots, count, rows, lanes), jnp.bfloat16),
            pltpu.VMEM((slots - 1, count * rows, lanes), jnp.bfloat16),
            pltpu.VMEM((count * rows, lanes), jnp.float32),
            pltpu.VMEM((count, rows, lanes), jnp.bfloat16),
            pltpu.VMEM((2, count, rows, lanes), jnp.bfloat16),
            pltpu.VMEM((count, slab), jnp.bfloat16),
            pltpu.VMEM((count, count * count // lanes, lanes), jnp.float32),
            pltpu.SemaphoreType.DMA((2, slots)),
            pltpu.SemaphoreType.DMA((3, count)),
            pltpu.SemaphoreType.DMA((3, count)),
        ],
        compiler_params=pltpu.CompilerParams(collective_id=0, has_side_effects=True),
        name="exchange",
    )(partners, orbitals, *consts)


def regrouped(value, count):
    bands, pairs = lax.axis_size("band"), lax.axis_size("pair")
    rows, lanes = value.shape
    value = value.reshape(bands, pairs, rows // count, lanes)
    value = lax.all_to_all(value, "band", split_axis=0, concat_axis=0, tiled=True)
    value = lax.all_to_all(value, "pair", split_axis=1, concat_axis=1, tiled=True)
    return value.reshape(count, rows * lanes // count)


def on_device(orbitals, partners):
    cells = orbitals.shape[1]
    size = round(cells ** (1.0 / 3.0))
    lanes = 2 * size
    count = lax.axis_size("band") * lax.axis_size("pair")
    consts = [jnp.asarray(table) for table in tables(size)]
    slab = cells // count
    small = count * count * count * 4 <= 2**24
    if small and slab % (8 * lanes) == 0 and count * count % (8 * lanes) == 0:
        return in_one_kernel(orbitals, partners, consts, count, lanes)
    own = orbitals.reshape(cells // lanes, lanes)
    live = partners[0]
    arrived = []
    for slot in range(partners.shape[1]):
        pairs = [(source, source ^ 2**slot) for source in range(lax.axis_size("band"))]
        arrived.append(lax.ppermute(own, "band", pairs))
    terms = []
    for slot in range(2):
        terms.append(slot_term(slot, live, own, arrived[slot], [], consts))
    applied = slot_term(2, live, own, arrived[2], terms, consts)
    phi, other = regrouped(own, count), regrouped(applied, count)
    partial = lax.dot_general(
        phi, other, (((1,), (1,)), ((), ())), preferred_element_type=jnp.float32
    )
    total = lax.psum(partial * (1.0 / cells), ("band", "pair"))
    removed = lax.dot_general(
        total, phi.astype(jnp.float32), (((0,), (0,)), ((), ())), precision=lax.Precision.HIGHEST
    )
    return other.astype(jnp.float32) - removed


def solution(mesh):
    placed = (P(("band", "pair"), None), P(("band", "pair"), None))
    return jax.shard_map(
        on_device, mesh=mesh, in_specs=placed, out_specs=P(None, ("band", "pair")), check_vma=False
    )
```

time: 102 us -> 69.2 us (0.68)
  starting transfers between devices: 14.1 us -> 0 us
  other arithmetic: 12.7 us -> 0 us
  waiting for transfers between devices: 12.7 us -> 0 us
  Pallas kernels: 55.3 us -> 66.7 us
  local copies, waits for them, and re-layouts: 6.67 us -> 2.26 us
    unnamed x1 -> x0, other arithmetic: 12.7 us -> none
    pallas_call x4 -> x1, Pallas kernels: 55.3 us -> 66.7 us  [in_one_kernel(): pl.pallas_call(functools.partial(whole_kernel, count, 1.0 / cells), out_s...]
    ppermute x3 -> x0, waiting for transfers between devices: 8.79 us -> none  [on_device(): arrived.append(lax.ppermute(own, 'band', pairs))]
    ppermute x3 -> x0, starting transfers between devices: 7.16 us -> none  [on_device(): arrived.append(lax.ppermute(own, 'band', pairs))]
    all_to_all x2 -> x0, starting transfers between devices: 6.96 us -> none  [the longest x1 3.49 us: regrouped(): lax.all_to_all(value, 'band', split_axis=0, concat_axis=0, tiled=True)]
    all_to_all x2 -> x0, waiting for transfers between devices: 3.88 us -> none  [the longest x1 3.88 us: regrouped(): lax.all_to_all(value, 'band', split_axis=0, concat_axis=0, tiled=True)]
    unnamed x8 -> x1, local copies, waits for them, and re-layouts: 5.79 us -> 2.26 us
  transfers between devices with their start and end apart: 5 -> 0, of which waited for: 3 -> 0; matrix products, arithmetic and copies ran while one was open for 1% -> 0% of each run, Pallas kernels for 25% -> 0%
where the time goes in v1:
time: 69.2 us; the launch traced here: 69 us
  Pallas kernels  66.7 us (96%)
  local copies, waits for them, and re-layouts  2.26 us (3%)
    pallas_call x1, Pallas kernels, in_one_kernel(): pl.pallas_call(functools.partial(whole_kernel, count, 1.0 / cells), out_s...  66.7 us
    unnamed x1, local copies, waits for them, and re-layouts  2.26 us

profile of v1, /device:TPU:0, one launch (start us, length us, event | category | flops | bytes accessed | tf_op | source)
XLA Modules:
  0.0 69.0 jit_solution(1826783954609528830)
XLA Ops:
  0.0 66.7 %exchange.1 = f32[32,8192]{1,0:T(8,128)} custom-call(s32[1,3]{1,0:T(1,128)} %live.1, bf16[1,262144]{1,0:T(2,128)(2,1)} %orbital.1, bf16[128,128]{1,0:T(8,128)(2,1)} %constant.12.clone.refs_0_, bf16[256,256]{1,0:T(8,128)(2,1)} %constant.13.clone.refs_1_, bf16[64,128]{1,0:T(8,128)(2,1)} %constant.14.clone.refs_2_, bf16[64,128]{1,0:T(8,128)(2,1)} %constant.15.clone.refs_3_, ...), custom_call_target="tpu_custom_call" | custom-call | tf_op jit(solution)/shard_map/exchange/pallas_call | solution.py:264
  66.7 2.3 %copy.10 = f32[32,8192]{1,0:T(8,128)} copy(f32[32,8192]{1,0:T(8,128)} %exchange.1) | data formatting | bytes 2097152

commit v2 on v1

--- a/solution.py
+++ b/solution.py
@@ -10,6 +10,7 @@
 
 screening = 0.05
 GROUP = 8
+CHUNKS = 4
 MESH = pl.DeviceIdType.MESH
 
 
@@ -79,7 +80,7 @@
     return pltpu.roll(field, size, 1) + field * sign.astype(jnp.float32)
 
 
-def solve(own, other, work, consts):
+def solve(own, other, work, consts, ready=None):
     left, right, forth, back, pair, along = consts
     lanes = work.shape[1]
     size, half = lanes // 2, lanes // 4
@@ -94,6 +95,8 @@
 
     for start in range(0, size, GROUP):
         rows = slice(start * half, (start + GROUP) * half)
+        if ready is not None:
+            ready(rows.start)
         field = own[rows, :].astype(jnp.float32) * other[rows, :].astype(jnp.float32)
         work[rows, :] = fold(middle(forth, spread(field, half), half))
     for start in range(0, half, GROUP):
@@ -111,7 +114,7 @@
 
 def finished(work, other, back, start):
     half = work.shape[1] // 4
-    rows = slice(start * half, (start + GROUP) * half)
+    rows = pl.ds(pl.multiple_of(start * half, GROUP * half), GROUP * half)
     field = middle(back, spread(fold(work[rows, :]), half), half)
     return rows, (field * other[rows, :].astype(jnp.float32)).astype(jnp.bfloat16)
 
@@ -154,43 +157,56 @@
     count, scale, live, orbital, *refs,
 ):
     consts, refs = refs[:6], refs[6:]
-    out, own, other, terms, work, applied, slabs, phi, sums, slot_sems, sent, came = refs
-    slots = other.shape[0]
+    total, phi, wide, own, other, terms, work, applied, slabs, sums, slot_sems, sent, came = refs
+    slots, chunks = slot_sems.shape[1:]
     rows, lanes = slabs.shape[2:]
     band, pair = lax.axis_index("band"), lax.axis_index("pair")
-    me = band * lax.axis_size("pair") + pair
-
-    def each(action):
-        lax.fori_loop(1, count, lambda step, _: (action(step), 0)[1], 0)
+    pairs = lax.axis_size("pair")
+    me = band * pairs + pair
+    last = slots - 1
+    stride = 2**last
+    side = lax.rem(band // stride, 2)
+
+    def each(number, action):
+        lax.fori_loop(1, number, lambda step, _: (action(step), 0)[1], 0)
 
     def peer_of(step):
         return lax.rem(me + step, count)
 
+    def near(step):
+        here = (band // (2 * stride) * stride + lax.rem(band, stride)) * pairs + pair
+        at = lax.rem(here + step, count // 2)
+        row = at // pairs
+        row = row // stride * (2 * stride) + side * stride + lax.rem(row, stride)
+        return row * pairs + lax.rem(at, pairs)
+
+    def across(index):
+        return index + (1 - 2 * side) * stride * pairs
+
     barrier = pltpu.get_barrier_semaphore()
-    each(lambda step: pl.semaphore_signal(
+    each(count, lambda step: pl.semaphore_signal(
         barrier, inc=1, device_id=place(peer_of(step)), device_id_type=MESH))
     grid = orbital[...].reshape(count * rows, lanes)
     own[...] = grid.reshape(count, rows, lanes)
     slabs[0, me] = own[me]
     pl.semaphore_wait(barrier, count - 1)
 
-    def fetch(slot):
-        stride = 2**slot
-        mate = band + stride - 2 * stride * lax.rem(band // stride, 2)
+    def fetch(slot, chunk):
+        far = 2**slot
+        mate = band + far - 2 * far * lax.rem(band // far, 2)
+        part = slice(chunk * count // chunks, (chunk + 1) * count // chunks)
         return pltpu.make_async_remote_copy(
-            src_ref=own, dst_ref=other.at[slot], send_sem=slot_sems.at[0, slot],
-            recv_sem=slot_sems.at[1, slot], device_id=(mate, pair), device_id_type=MESH,
-        )
-
-    def regroup(which, source):
-        def copy(step):
-            peer = peer_of(step)
-            return pltpu.make_async_remote_copy(
-                src_ref=source.at[peer], dst_ref=slabs.at[which, me],
-                send_sem=sent.at[which, step], recv_sem=came.at[which, step],
-                device_id=place(peer), device_id_type=MESH,
-            )
-        return copy
+            src_ref=own.at[part], dst_ref=other.at[slot, part],
+            send_sem=slot_sems.at[0, slot, chunk], recv_sem=slot_sems.at[1, slot, chunk],
+            device_id=(mate, pair), device_id_type=MESH,
+        )
+
+    def send(source, which, peer, origin, queue):
+        return pltpu.make_async_remote_copy(
+            src_ref=source.at[peer], dst_ref=slabs.at[which, origin],
+            send_sem=sent.at[queue, peer], recv_sem=came.at[which, origin],
+            device_id=place(peer), device_id_type=MESH,
+        )
 
     def share(step):
         return pltpu.make_async_remote_copy(
@@ -198,61 +214,83 @@
             recv_sem=came.at[2, step], device_id=place(peer_of(step)), device_id_type=MESH,
         )
 
-    def widen(which):
+    def widen(which, result):
         work[...] = slabs[which].reshape(count * rows, lanes).astype(jnp.float32)
-        return [work[pl.ds(row, count, stride=rows), :] for row in range(rows)]
-
-    fetches = [fetch(slot) for slot in range(slots)]
-    for copy in fetches:
-        copy.start()
-    first, second = regroup(0, own), regroup(1, applied)
-    each(lambda step: first(step).start())
-    planes = lanes // 2
+        for row in range(rows):
+            value = work[pl.ds(row, count, stride=rows), :]
+            result[:, row * lanes : (row + 1) * lanes] = value.astype(result.dtype)
+
+    fetches = [[fetch(slot, chunk) for chunk in range(chunks)] for slot in range(slots)]
+    for copies in fetches:
+        for copy in copies:
+            copy.start()
+    each(count // 2, lambda step: send(own, 0, near(step), me, 0).start())
+    groups = lanes // 2 // GROUP
+    blocks = count // groups
     flat = own.reshape(count * rows, lanes)
     for slot in range(slots):
-        fetches[slot].wait()
         mate = other.at[slot].reshape(count * rows, lanes)
-        solve(flat, mate, work, consts)
-        for start in range(0, planes, GROUP):
-            span, term = finished(work, mate, consts[3], start)
+
+        def ready(row, slot=slot):
+            chunk, rest = divmod(row, count * rows // chunks)
+            if rest == 0:
+                fetches[slot][chunk].wait()
+                if slot == last and chunk == chunks - 1:
+                    slabs[0, across(me)] = other[last, me]
+                    each(count // 2, lambda step: send(
+                        other.at[last], 0, near(step), across(me), 3).start())
+
+        solve(flat, mate, work, consts, ready)
+        for group in range(groups):
+            if slot == last:
+                group = lax.rem(me // blocks + groups // 2 + group, groups)
+            span, term = finished(work, mate, consts[3], group * GROUP)
             term = jnp.where(live[0, slot] >= 0, term.astype(jnp.float32), 0.0)
-            if slot + 1 < slots:
+            if slot < last:
                 terms[slot, span, :] = term.astype(jnp.bfloat16)
                 continue
-            total = terms[0, span, :].astype(jnp.float32)
-            for earlier in range(1, slots - 1):
-                total = total + terms[earlier, span, :].astype(jnp.float32)
-            total = (total + term).astype(jnp.bfloat16)
-            blocks = (span.stop - span.start) // rows
-            at = span.start // rows
-            applied[at : at + blocks] = total.reshape(blocks, rows, lanes)
+            ahead = terms[0, span, :].astype(jnp.float32)
+            for earlier in range(1, last):
+                ahead = ahead + terms[earlier, span, :].astype(jnp.float32)
+            ahead = (ahead + term).astype(jnp.bfloat16)
+            applied[pl.ds(group * blocks, blocks)] = ahead.reshape(blocks, rows, lanes)
+            for block in range(blocks):
+                target = group * blocks + block
+
+                @pl.when(target != me)
+                def _(target=target):
+                    send(applied, 1, target, me, 1).start()
+
     slabs[1, me] = applied[me]
-    each(lambda step: second(step).start())
-    each(lambda step: first(step).wait())
-    for row, value in enumerate(widen(0)):
-        phi[:, row * lanes : (row + 1) * lanes] = value.astype(jnp.bfloat16)
-    each(lambda step: second(step).wait())
-    for row, value in enumerate(widen(1)):
-        out[:, row * lanes : (row + 1) * lanes] = value
+
+    def arrived(step):
+        send(own, 0, near(step), near(step), 0).wait()
+        send(other.at[last], 0, near(step), across(near(step)), 3).wait()
+
+    each(count // 2, arrived)
+    widen(0, phi)
+    each(count, lambda step: send(applied, 1, peer_of(step), peer_of(step), 1).wait())
+    widen(1, wide)
     partial = lax.dot_general(
-        phi[...], out[...].astype(jnp.bfloat16), (((1,), (1,)), ((), ())),
-        preferred_element_type=jnp.float32,
+        phi[...], wide[...], (((1,), (1,)), ((), ())), preferred_element_type=jnp.float32
     ) * scale
     short = count * count // lanes
     sums[me] = jnp.concatenate(
         [partial[at : at + short] for at in range(0, count, short)], axis=1
     )
-    each(lambda step: share(step).start())
-    each(lambda step: share(step).wait())
+    each(count, lambda step: share(step).start())
+    each(count, lambda step: share(step).wait())
     packed = jnp.sum(sums[...], axis=0)
-    total = jnp.concatenate(
+    total[...] = jnp.concatenate(
         [packed[:, at : at + count] for at in range(0, lanes, count)], axis=0
     )
+
+
+def projected(total, phi, applied):
     removed = lax.dot_general(
-        total, phi[...].astype(jnp.float32), (((0,), (0,)), ((), ())),
-        precision=lax.Precision.HIGHEST, preferred_element_type=jnp.float32,
-    )
-    out[...] = out[...] - removed
+        total, phi.astype(jnp.float32), (((0,), (0,)), ((), ())), precision=lax.Precision.HIGHEST
+    )
+    return applied.astype(jnp.float32) - removed
 
 
 def in_one_kernel(orbitals, partners, consts, count, lanes):
@@ -261,11 +299,15 @@
     slab = cells // count
     rows = slab // lanes
     vmem = pl.BlockSpec(memory_space=pltpu.VMEM)
-    return pl.pallas_call(
+    total, phi, wide = pl.pallas_call(
         functools.partial(whole_kernel, count, 1.0 / cells),
-        out_shape=jax.ShapeDtypeStruct((count, slab), jnp.float32),
+        out_shape=[
+            jax.ShapeDtypeStruct((count, count), jnp.float32),
+            jax.ShapeDtypeStruct((count, slab), jnp.bfloat16),
+            jax.ShapeDtypeStruct((count, slab), jnp.bfloat16),
+        ],
         in_specs=[pl.BlockSpec(memory_space=pltpu.SMEM)] + [vmem] * (1 + len(consts)),
-        out_specs=vmem,
+        out_specs=[vmem] * 3,
         scratch_shapes=[
             pltpu.VMEM((count, rows, lanes), jnp.bfloat16),
             pltpu.VMEM((slots, count, rows, lanes), jnp.bfloat16),
@@ -273,15 +315,15 @@
             pltpu.VMEM((count * rows, lanes), jnp.float32),
             pltpu.VMEM((count, rows, lanes), jnp.bfloat16),
             pltpu.VMEM((2, count, rows, lanes), jnp.bfloat16),
-            pltpu.VMEM((count, slab), jnp.bfloat16),
             pltpu.VMEM((count, count * count // lanes, lanes), jnp.float32),
-            pltpu.SemaphoreType.DMA((2, slots)),
-            pltpu.SemaphoreType.DMA((3, count)),
+            pltpu.SemaphoreType.DMA((2, slots, CHUNKS)),
+            pltpu.SemaphoreType.DMA((4, count)),
             pltpu.SemaphoreType.DMA((3, count)),
         ],
         compiler_params=pltpu.CompilerParams(collective_id=0, has_side_effects=True),
         name="exchange",
     )(partners, orbitals, *consts)
+    return projected(total, phi, wide)
 
 
 def regrouped(value, count):
@@ -318,10 +360,7 @@
         phi, other, (((1,), (1,)), ((), ())), preferred_element_type=jnp.float32
     )
     total = lax.psum(partial * (1.0 / cells), ("band", "pair"))
-    removed = lax.dot_general(
-        total, phi.astype(jnp.float32), (((0,), (0,)), ((), ())), precision=lax.Precision.HIGHEST
-    )
-    return other.astype(jnp.float32) - removed
+    return projected(total, phi, other)
 
 
 def solution(mesh):

time: 69.2 us -> 65.6 us (0.948)
  Pallas kernels: 66.7 us -> 62.6 us
  matrix products: 0 us -> 2.82 us
  local copies, waits for them, and re-layouts: 2.26 us -> 0 us
    pallas_call x1, Pallas kernels: 66.7 us -> 62.6 us  [in_one_kernel(): pl.pallas_call(functools.partial(whole_kernel, count, 1.0 / cells), out_s...]
    dot_general x0 -> x1, matrix products: none -> 2.82 us  [projected(): lax.dot_general(total, phi.astype(jnp.float32), (((0,), (0,)), ((), ())),...]
    unnamed x1 -> x0, local copies, waits for them, and re-layouts: 2.26 us -> none
where the time goes in v2:
time: 65.6 us; the launch traced here: 65.5 us
  Pallas kernels  62.6 us (95%)
  matrix products  2.82 us (4%)
    pallas_call x1, Pallas kernels, in_one_kernel(): pl.pallas_call(functools.partial(whole_kernel, count, 1.0 / cells), out_s...  62.6 us
    dot_general x1, matrix products, projected(): lax.dot_general(total, phi.astype(jnp.float32), (((0,), (0,)), ((), ())),...  2.82 us

profile of v2, /device:TPU:0, one launch (start us, length us, event | category | flops | bytes accessed | tf_op | source)
XLA Modules:
  0.0 65.5 jit_solution(17788885427927027366)
XLA Ops:
  0.0 62.6 %exchange.1 = (f32[32,32]{1,0:T(8,128)}, bf16[32,8192]{1,0:T(8,128)(2,1)}, bf16[32,8192]{1,0:T(8,128)(2,1)}) custom-call(s32[1,3]{1,0:T(1,128)} %live.1, bf16[1,262144]{1,0:T(2,128)(2,1)} %orbital.1, bf16[128,128]{1,0:T(8,128)(2,1)} %constant.12.clone.refs_0_, bf16[256,256]{1,0:T(8,128)(2,1)} %constant.13.clone.refs_1_, ...), custom_call_target="tpu_custom_call" | custom-call | tf_op jit(solution)/shard_map/exchange/pallas_call | solution.py:302
  62.6 2.8 %convolution_subtract_fusion = f32[32,8192]{1,0:T(8,128)} fusion(f32[32,32]{1,0:T(8,128)} %get-tuple-element.9, bf16[32,8192]{1,0:T(8,128)(2,1)} %get-tuple-element.10, bf16[32,8192]{1,0:T(8,128)(2,1)} %get-tuple-element.8), kind=kOutput, calls=%fused_computation | convolution fusion | flops 101187584 | bytes 2101248 | tf_op jit(solution)/shard_map/dot_general | solution.py:290

commit v3 on v2

--- a/solution.py
+++ b/solution.py
@@ -288,7 +288,7 @@
 
 def projected(total, phi, applied):
     removed = lax.dot_general(
-        total, phi.astype(jnp.float32), (((0,), (0,)), ((), ())), precision=lax.Precision.HIGHEST
+        total, phi.astype(jnp.float32), (((0,), (0,)), ((), ())), precision=lax.Precision.HIGH
     )
     return applied.astype(jnp.float32) - removed
 

time: 65.6 us -> 65.5 us (level)
  no operation moved by 1% of the time
where the time goes in v3:
time: 65.5 us; the launch traced here: 65.3 us
  Pallas kernels  62.6 us (96%)
  matrix products  2.67 us (4%)
    pallas_call x1, Pallas kernels, in_one_kernel(): pl.pallas_call(functools.partial(whole_kernel, count, 1.0 / cells), out_s...  62.6 us
    dot_general x1, matrix products, projected(): lax.dot_general(total, phi.astype(jnp.float32), (((0,), (0,)), ((), ())),...  2.67 us

profile of v3, /device:TPU:0, one launch (start us, length us, event | category | flops | bytes accessed | tf_op | source)
XLA Modules:
  0.0 65.3 jit_solution(2458352661298570315)
XLA Ops:
  0.0 62.6 %exchange.1 = (f32[32,32]{1,0:T(8,128)}, bf16[32,8192]{1,0:T(8,128)(2,1)}, bf16[32,8192]{1,0:T(8,128)(2,1)}) custom-call(s32[1,3]{1,0:T(1,128)} %live.1, bf16[1,262144]{1,0:T(2,128)(2,1)} %orbital.1, bf16[128,128]{1,0:T(8,128)(2,1)} %constant.12.clone.refs_0_, bf16[256,256]{1,0:T(8,128)(2,1)} %constant.13.clone.refs_1_, ...), custom_call_target="tpu_custom_call" | custom-call | tf_op jit(solution)/shard_map/exchange/pallas_call | solution.py:302
  62.6 2.7 %convolution_subtract_fusion = f32[32,8192]{1,0:T(8,128)} fusion(f32[32,32]{1,0:T(8,128)} %get-tuple-element.9, bf16[32,8192]{1,0:T(8,128)(2,1)} %get-tuple-element.10, bf16[32,8192]{1,0:T(8,128)(2,1)} %get-tuple-element.8), kind=kOutput, calls=%fused_computation | convolution fusion | flops 50855936 | bytes 2101248 | tf_op jit(solution)/shard_map/dot_general | solution.py:290
